TPU v7x, 32 devices: a whole 2x2x4 slice. The times are simulated.
32 devices in a mesh: row: 4 (over z), col: 8 (over y, x, core).
Axes of the slice: x: 2, y: 2, z: 4, core: 2. Of those that a mesh axis runs over, the one named last changes fastest.
Arguments:
- tokens: bfloat16 [256, 8192], P('col', 'row'), may hold values from -6 to 6
- out_grad: bfloat16 [256, 8192], P('col', 'row'), may hold values from -1.1953125 to 1.1953125
- w_gate: bfloat16 [8192, 16384], P('row', 'col'), may hold values from -0.0625 to 0.0625
- w_up: bfloat16 [8192, 16384], P('row', 'col'), may hold values from -0.0625 to 0.0625
- w_down: bfloat16 [16384, 8192], P('col', 'row'), may hold values from -0.046875 to 0.046875
Outputs:
- grad_input: bfloat16 [256, 8192], P('col', 'row')
- grad_gate: bfloat16 [8192, 16384], P('row', 'col')
- grad_up: bfloat16 [8192, 16384], P('row', 'col')
- grad_down: bfloat16 [16384, 8192], P('col', 'row')
All inputs are finite; a program needn't handle non-finite values.
Results may differ from a plain program's by a relative error of at most 0.0049.
Values may be sent and summed in bfloat16 or wider, within the bound.
A program may use at most 128 MiB of HBM per device.

v0:
```python
import jax
import jax.numpy as jnp
from jax import lax
from jax.sharding import PartitionSpec as P


def contract(left_array, right_array, left_dim, right_dim):
    return lax.dot_general(
        left_array,
        right_array,
        (((left_dim,), (right_dim,)), ((), ())),
        preferred_element_type=jnp.float32,
    )


def swiglu_back(gate_sum, up_sum, hidden_grad):
    logistic = jax.nn.sigmoid(gate_sum)
    active = gate_sum * logistic
    hidden = (active * up_sum).astype(jnp.bfloat16)
    up_grad = (hidden_grad * active).astype(jnp.bfloat16)
    gate_grad = (hidden_grad * up_sum * logistic * (1.0 + gate_sum * (1.0 - logistic))).astype(
        jnp.bfloat16
    )
    return (hidden, gate_grad, up_grad)


def shards(tokens, out_grad, w_gate, w_up, w_down):
    all_tokens, all_grads = (
        lax.all_gather(tokens, "col", axis=0, tiled=True),
        lax.all_gather(out_grad, "col", axis=0, tiled=True),
    )
    gate_part = jnp.dot(all_tokens, w_gate, preferred_element_type=jnp.float32)
    up_part = jnp.dot(all_tokens, w_up, preferred_element_type=jnp.float32)
    grad_part = contract(all_grads, w_down, 1, 1)
    gate_sum, up_sum, hidden_grad = lax.psum((gate_part, up_part, grad_part), "row")
    hidden, gate_grad, up_grad = swiglu_back(gate_sum, up_sum, hidden_grad)
    grad_down = contract(hidden, all_grads, 0, 0).astype(jnp.bfloat16)
    grad_gate = contract(all_tokens, gate_grad, 0, 0).astype(jnp.bfloat16)
    grad_up = contract(all_tokens, up_grad, 0, 0).astype(jnp.bfloat16)
    grad_input = lax.psum_scatter(
        contract(gate_grad, w_gate, 1, 1) + contract(up_grad, w_up, 1, 1),
        "col",
        scatter_dimension=0,
        tiled=True,
    ).astype(jnp.bfloat16)
    return (grad_input, grad_gate, grad_up, grad_down)


def solution(mesh):
    return jax.shard_map(
        shards,
        mesh=mesh,
        in_specs=(
            P("col", "row"),
            P("col", "row"),
            P("row", "col"),
            P("row", "col"),
            P("col", "row"),
        ),
        out_specs=(P("col", "row"), P("row", "col"), P("row", "col"), P("col", "row")),
        check_vma=False,
    )
```

profile of v0, /device:TPU:0, one launch (start us, length us, event | category | flops | bytes accessed | tf_op | source)
XLA Modules:
  0.0 358.6 jit_solution(17293567438412855465)
XLA Ops:
  7.2 0.0 all-gather.5.cloned.1.call-start
  7.2 0.7 all-gather.5.cloned.1.call-update
  7.9 0.0 all-gather.3.cloned.1.call-start
  7.9 0.7 all-gather.3.cloned.1.call-update
  8.6 0.0 all-reduce.3.cloned.1.call-start
  8.7 27.4 %all-gather.5.cloned.1.call-done = bf16[256,2048]{1,0:T(8,128)(2,1)} async-done(((bf16[32,2048]{1,0:T(8,128)(2,1)}), bf16[256,2048]{1,0:T(8,128)(2,1)}) %all-gather.5.cloned.1.call-update) | async-done | bytes 1048592 | tf_op jit(solution)/shard_map/all_gather | solution.py:29
  36.1 0.0 copy-start
  36.1 7.4 %fusion.5 = f32[256,2048]{1,0:T(8,128)} fusion(bf16[256,2048]{1,0:T(8,128)(2,1)} %all-gather.5.cloned.1.call-done, bf16[2048,2048]{1,0:T(8,128)(2,1)} %param.7), kind=kOutput, calls=%fused_computation.12 | convolution fusion | flops 2147483648 | bytes 11534336 | tf_op jit(solution)/shard_map/dot_general | solution.py:32
  43.5 0.0 copy-done
  43.6 7.2 %fusion.4 = f32[256,2048]{1,0:T(8,128)} fusion(bf16[256,2048]{1,0:T(8,128)(2,1)S(1)} %copy-done, bf16[2048,2048]{1,0:T(8,128)(2,1)} %param.8), kind=kOutput, calls=%fused_computation.11 | convolution fusion | flops 2147483648 | bytes 11534336 | tf_op jit(solution)/shard_map/dot_general | solution.py:33
  50.7 10.8 %all-gather.3.cloned.1.call-done = bf16[256,2048]{1,0:T(8,128)(2,1)} async-done(((bf16[32,2048]{1,0:T(8,128)(2,1)}), bf16[256,2048]{1,0:T(8,128)(2,1)}) %all-gather.3.cloned.1.call-update) | async-done | bytes 1048592 | tf_op jit(solution)/shard_map/all_gather | solution.py:30
  61.5 7.4 %fusion.3 = f32[256,2048]{1,0:T(8,128)} fusion(bf16[256,2048]{1,0:T(8,128)(2,1)} %all-gather.3.cloned.1.call-done, bf16[2048,2048]{1,0:T(8,128)(2,1)} %param.9), kind=kOutput, calls=%fused_computation.10 | convolution fusion | flops 2147483648 | bytes 11534336 | tf_op jit(solution)/shard_map/dot_general | solution.py:8
  68.9 0.0 all-reduce.3.cloned.1.call-update
  68.9 0.2 reduce-scatter.2.cloned.1.call-start
  69.2 223.5 %all-reduce.3.cloned.1.call-done = (f32[256,2048]{1,0:T(8,128)}, f32[256,2048]{1,0:T(8,128)}, f32[256,2048]{1,0:T(8,128)}) async-done(((f32[256,2048]{1,0:T(8,128)}, f32[256,2048]{1,0:T(8,128)}, f32[256,2048]{1,0:T(8,128)}), (f32[256,2048]{1,0:T(8,128)}, f32[256,2048]{1,0:T(8,128)}, f32[256,2048]{1,0:T(8,128)})) %all-reduce.3.cloned.1.call-update) | async-done | bytes 6291472 | tf_op jit(solution)/shard_map/psum | solution.py:35
  292.6 0.0 slice-start
  292.6 4.3 %multiply_convert_fusion.1 = (bf16[256,2048]{1,0:T(8,128)(2,1)S(1)}, bf16[256,2048]{1,0:T(8,128)(2,1)S(1)}) fusion(f32[256,2048]{1,0:T(8,128)} %get-tuple-element.9, f32[256,2048]{1,0:T(8,128)} %get-tuple-element.8, f32[256,2048]{1,0:T(8,128)} %get-tuple-element.10), kind=kLoop, calls=%fused_computation.5 | loop fusion | flops 6815744 | bytes 8388608 | tf_op jit(solution)/shard_map/convert_element_type | solution.py:20
  297.0 0.0 slice-start.1
  297.0 5.9 %fusion.6 = f32[256,2048]{1,0:T(8,128)S(1)} fusion(bf16[256,2048]{1,0:T(8,128)(2,1)S(1)} %get-tuple-element.12, bf16[2048,2048]{1,0:T(8,128)(2,1)} %param.7), kind=kOutput, calls=%fused_computation.13 | convolution fusion | flops 2147483648 | bytes 11534336 | tf_op jit(solution)/shard_map/dot_general | solution.py:8
  302.9 0.0 slice-done
  302.9 0.0 slice-done.1
  302.9 3.7 %convolution_add_fusion = f32[256,2048]{1,0:T(8,128)} fusion(f32[256,2048]{1,0:T(8,128)S(1)} %fusion.6, bf16[256,2048]{1,0:T(8,128)(2,1)S(1)} %get-tuple-element.11, bf16[2048,2048]{1,0:T(8,128)(2,1)S(1)} %bitcast.20), kind=kOutput, calls=%fused_computation.3 | convolution fusion | flops 2148007936 | bytes 13631488 | tf_op jit(solution)/shard_map/dot_general | solution.py:8
  306.6 0.0 reduce-scatter.2.cloned.1.call-update
  306.6 5.8 %convert_bitcast_fusion.1 = bf16[2048,2048]{0,1:T(8,128)(2,1)} fusion(bf16[256,2048]{1,0:T(8,128)(2,1)S(1)} %get-tuple-element.12, bf16[256,2048]{1,0:T(8,128)(2,1)S(1)} %copy-done), kind=kOutput, calls=%fused_computation.1 | convolution fusion | flops 2151677952 | bytes 10485760 | tf_op jit(solution)/shard_map/dot_general | solution.py:8
  312.4 12.4 %copy.9 = bf16[2048,2048]{1,0:T(8,128)(2,1)} copy(bf16[2048,2048]{0,1:T(8,128)(2,1)} %convert_bitcast_fusion.1) | data formatting | bytes 16777216
  324.8 5.8 %convert_bitcast_fusion = bf16[2048,2048]{0,1:T(8,128)(2,1)} fusion(bf16[256,2048]{1,0:T(8,128)(2,1)S(1)} %get-tuple-element.11, bf16[256,2048]{1,0:T(8,128)(2,1)S(1)} %copy-done), kind=kOutput, calls=%fused_computation | convolution fusion | flops 2151677952 | bytes 10485760 | tf_op jit(solution)/shard_map/dot_general | solution.py:8
  330.6 0.0 copy-start.1
  330.6 0.0 copy-start.2
  330.6 12.4 %copy.10 = bf16[2048,2048]{1,0:T(8,128)(2,1)} copy(bf16[2048,2048]{0,1:T(8,128)(2,1)} %convert_bitcast_fusion) | data formatting | bytes 16777216
  343.0 0.0 copy-done.1
  343.0 0.0 copy-done.2
  343.0 7.5 %convolution_convert_fusion = bf16[2048,2048]{1,0:T(8,128)(2,1)} fusion(bf16[256,2048]{1,0:T(8,128)(2,1)S(1)} %copy-done.2, f32[256,2048]{1,0:T(8,128)} %get-tuple-element.10, f32[256,2048]{1,0:T(8,128)S(1)} %copy-done.1), kind=kOutput, calls=%fused_computation.2 | convolution fusion | flops 2154823680 | bytes 13631488 | tf_op jit(solution)/shard_map/dot_general | solution.py:8
  350.5 0.0 reduce-scatter.2.cloned.1.call-done
  350.5 1.6 convert_element_type.29
  (1 shorter events, 0.0 us)
Async XLA Ops:
  7.2 28.9 %all-gather.5.cloned.1.call-start = ((), (), s32[]{:S(2)}) async-start(), calls=%async_computation.2 | async-start | bytes 1179648 | tf_op jit(solution)/shard_map/all_gather | solution.py:29
  7.9 53.6 %all-gather.3.cloned.1.call-start = ((), (), s32[]{:S(2)}) async-start(), calls=%async_computation.1 | async-start | bytes 1179648 | tf_op jit(solution)/shard_map/all_gather | solution.py:30
  8.6 284.0 %all-reduce.3.cloned.1.call-start = ((), (), s32[]{:S(2)}) async-start(), calls=%async_computation.4 | async-start | bytes 12582912 | tf_op jit(solution)/shard_map/psum | solution.py:35
  36.1 7.4 %copy-start = (bf16[256,2048]{1,0:T(8,128)(2,1)S(1)}, bf16[256,2048]{1,0:T(8,128)(2,1)}, u32[]{:S(2)}) copy-start(bf16[256,2048]{1,0:T(8,128)(2,1)} %all-gather.5.cloned.1.call-done) | copy-start | bytes 3145732
  68.9 281.5 %reduce-scatter.2.cloned.1.call-start = ((), (), s32[]{:S(2)}) async-start(), calls=%async_computation.3 | async-start | bytes 2359296 | tf_op jit(solution)/shard_map/reduce_scatter | solution.py:40
  292.6 10.2 %slice-start = ((s8[8388608]{0:T(1024)(128)(4,1)}), s8[4194304]{0:T(1024)(128)(4,1)S(1)}, s32[]{:S(2)}) async-start(s8[8388608]{0:T(1024)(128)(4,1)} %bitcast.19), calls=%async_computation.5 | async-start | bytes 8388608
  297.0 5.9 %slice-start.1 = ((s8[8388608]{0:T(1024)(128)(4,1)}), s8[4194304]{0:T(1024)(128)(4,1)S(1)}, s32[]{:S(2)}) async-start(s8[8388608]{0:T(1024)(128)(4,1)} %bitcast.19), calls=%async_computation.6 | async-start | bytes 8388608
  330.6 12.4 %copy-start.1 = (f32[256,2048]{1,0:T(8,128)S(1)}, f32[256,2048]{1,0:T(8,128)}, u32[]{:S(2)}) copy-start(f32[256,2048]{1,0:T(8,128)} %get-tuple-element.8) | copy-start | bytes 6291460
  330.6 12.4 %copy-start.2 = (bf16[256,2048]{1,0:T(8,128)(2,1)S(1)}, bf16[256,2048]{1,0:T(8,128)(2,1)}, u32[]{:S(2)}) copy-start(bf16[256,2048]{1,0:T(8,128)(2,1)} %all-gather.3.cloned.1.call-done) | copy-start | bytes 3145732
Sparse Core Ops, SparseCore 0:
  9.9 26.1 all-gather.4
  38.0 23.4 all-gather.2
  69.1 223.5 all-reduce.2
  306.8 40.1 reduce-scatter.1
where the time goes:
time: 359 us
  waiting for transfers between devices  263 us (73%)
  matrix products  50.7 us (14%)
  local copies, waits for them, and re-layouts  24.8 us (7%)
  between operations  13.8 us (4%)
  other arithmetic  5.93 us (2%)
    psum x1, waiting for transfers between devices, shards(): lax.psum((gate_part, up_part, grad_part), 'row')  223 us
    dot_general x6, matrix products, contract(): lax.dot_general(left_array, right_array, (((left_dim,), (right_dim,)), ((...  36 us
    all_gather x1, waiting for transfers between devices, shards(): lax.all_gather(tokens, 'col', axis=0, tiled=True)  27.4 us
    unnamed x12, local copies, waits for them, and re-layouts  24.8 us
    all_gather x1, waiting for transfers between devices, shards(): lax.all_gather(out_grad, 'col', axis=0, tiled=True)  10.8 us
    dot_general x1, matrix products, shards(): gate_part = jnp.dot(all_tokens, w_gate, preferred_element_type=jnp.float32)  7.44 us
  transfers between devices with their start and end apart: 4, of which 3 were waited for; matrix products, arithmetic and copies ran while one was open for 16% of the time, Pallas kernels for 0%

commit v1 on v0

--- a/solution.py
+++ b/solution.py
@@ -1,7 +1,45 @@
+import functools
 import jax
 import jax.numpy as jnp
 from jax import lax
 from jax.sharding import PartitionSpec as P
+from jax.lax import axis_index, axis_size, ppermute
+
+
+def get_core(arr, peer_axis):
+    new = axis_size(peer_axis)
+    z1 = axis_index(peer_axis)
+    u_next, carry_out, outer = (new, z1, arr.shape[0])
+    column = []
+    d = 0
+    while d < u_next:
+        column.append((d, (d + 1) % u_next))
+        d += 1
+    block_list = []
+    d = 0
+    while d < u_next:
+        block_list.append((d, (d - 1) % u_next))
+        d = d + 1
+    block_out = jnp.zeros((*arr.shape[:0], u_next * outer, *arr.shape[1:]), arr.dtype)
+    block_out = lax.dynamic_update_slice_in_dim(block_out, arr, carry_out * outer, axis=0)
+    t_next = earlier = arr
+    g_now = u_next // 2
+    j = 1
+    while j < g_now + 1:
+        t_next = ppermute(t_next, peer_axis, column)
+        block_out = lax.dynamic_update_slice_in_dim(
+            block_out, t_next, (carry_out - j) % u_next * outer, axis=0
+        )
+        if j < u_next - g_now:
+            earlier = ppermute(earlier, peer_axis, block_list)
+            block_out = lax.dynamic_update_slice_in_dim(
+                block_out, earlier, (carry_out + j) % u_next * outer, axis=0
+            )
+        j = j + 1
+    return block_out
+
+
+form_cube = functools.partial(get_core, peer_axis="col")
 
 
 def contract(left_array, right_array, left_dim, right_dim):
@@ -25,10 +63,7 @@
 
 
 def shards(tokens, out_grad, w_gate, w_up, w_down):
-    all_tokens, all_grads = (
-        lax.all_gather(tokens, "col", axis=0, tiled=True),
-        lax.all_gather(out_grad, "col", axis=0, tiled=True),
-    )
+    all_tokens, all_grads = (lax.all_gather(tokens, "col", axis=0, tiled=True), form_cube(out_grad))
     gate_part = jnp.dot(all_tokens, w_gate, preferred_element_type=jnp.float32)
     up_part = jnp.dot(all_tokens, w_up, preferred_element_type=jnp.float32)
     grad_part = contract(all_grads, w_down, 1, 1)

time: 359 us -> 346 us (0.964)
  waiting for transfers between devices: 263 us -> 239 us
  starting transfers between devices: 0.34 us -> 9.23 us
    all_gather x1, waiting for transfers between devices: 27.4 us -> 0.01 us  [shards(): lax.all_gather(tokens, 'col', axis=0, tiled=True)]
    ppermute x0 -> x7, waiting for transfers between devices: none -> 13.5 us  [the longest x4 12.8 us: get_core(): t_next = ppermute(t_next, peer_axis, column)]
    all_gather x1 -> x0, waiting for transfers between devices: 10.8 us -> none  [shards(): lax.all_gather(out_grad, 'col', axis=0, tiled=True)]
    ppermute x0 -> x7, starting transfers between devices: none -> 8.93 us  [the longest x3 8.42 us: get_core(): earlier = ppermute(earlier, peer_axis, block_list)]
    unnamed x12 -> x14, local copies, waits for them, and re-layouts: 24.8 us -> 25.8 us
  transfers between devices with their start and end apart: 4 -> 10, of which waited for: 3 -> 7; matrix products, arithmetic and copies ran while one was open for 16% -> 15% of each run, Pallas kernels for 0% -> 0%
where the time goes in v1:
time: 346 us; the launch traced here: 345 us
  waiting for transfers between devices  239 us (69%)
  matrix products  50.2 us (15%)
  local copies, waits for them, and re-layouts  26.9 us (8%)
  between operations  14 us (4%)
  starting transfers between devices  9.23 us (3%)
  other arithmetic  5.93 us (2%)
    psum x1, waiting for transfers between devices, shards(): lax.psum((gate_part, up_part, grad_part), 'row')  225 us
    dot_general x6, matrix products, contract(): lax.dot_general(left_array, right_array, (((left_dim,), (right_dim,)), ((...  35.7 us
    unnamed x14, local copies, waits for them, and re-layouts  25.8 us
    ppermute x4, waiting for transfers between devices, get_core(): t_next = ppermute(t_next, peer_axis, column)  12.8 us
    ppermute x3, starting transfers between devices, get_core(): earlier = ppermute(earlier, peer_axis, block_list)  8.42 us
    dot_general x1, matrix products, shards(): gate_part = jnp.dot(all_tokens, w_gate, preferred_element_type=jnp.float32)  7.44 us
    dot_general x1, matrix products, shards(): up_part = jnp.dot(all_tokens, w_up, preferred_element_type=jnp.float32)  7.03 us
  transfers between devices with their start and end apart: 10, of which 7 were waited for; matrix products, arithmetic and copies ran while one was open for 15% of the time, Pallas kernels for 0%

profile of v1, /device:TPU:0, one launch (start us, length us, event | category | flops | bytes accessed | tf_op | source)
XLA Modules:
  0.0 345.1 jit_solution(4803818524556609871)
XLA Ops:
  7.2 0.0 all-gather.2.cloned.1.call-start
  7.2 0.5 collective-permute-start
  7.7 2.9 collective-permute-start.1
  10.7 0.0 all-gather.2.cloned.1.call-update
  10.7 0.0 all-reduce.3.cloned.1.call-start
  10.9 0.1 broadcast_in_dim.3
  11.0 0.9 constant_dynamic-update-slice_fusion.7
  11.9 1.5 collective-permute-done
  13.5 0.0 collective-permute-start.2
  13.5 0.4 collective-permute-done.1
  13.8 2.7 collective-permute-start.3
  16.6 2.2 collective-permute-done.2
  18.8 0.0 collective-permute-start.4
  18.8 0.3 collective-permute-done.3
  19.1 2.8 collective-permute-start.5
  21.9 3.9 %collective-permute-done.4 = bf16[32,2048]{1,0:T(8,128)(2,1)S(1)} collective-permute-done((bf16[32,2048]{1,0:T(8,128)(2,1)S(1)}, bf16[32,2048]{1,0:T(8,128)(2,1)S(1)}, u32[]{:S(2)}, u32[]{:S(2)}) %collective-permute-start.4) | collective-permute-done | bytes 131104 | tf_op jit(solution)/shard_map/ppermute | solution.py:29
  25.7 0.0 collective-permute-start.6
  25.7 0.0 collective-permute-done.5
  25.8 5.2 %collective-permute-done.6 = bf16[32,2048]{1,0:T(8,128)(2,1)S(1)} collective-permute-done((bf16[32,2048]{1,0:T(8,128)(2,1)S(1)}, bf16[32,2048]{1,0:T(8,128)(2,1)S(1)}, u32[]{:S(2)}, u32[]{:S(2)}) %collective-permute-start.6) | collective-permute-done | bytes 131104 | tf_op jit(solution)/shard_map/ppermute | solution.py:29
  31.0 0.0 copy-start.2
  31.0 1.0 copy-done.2
  32.0 7.1 %fusion.3 = f32[256,2048]{1,0:T(8,128)} fusion(bf16[256,2048]{1,0:T(8,128)(2,1)S(1)} %constant_dynamic-update-slice_fusion, bf16[2048,2048]{1,0:T(8,128)(2,1)} %param.9), kind=kOutput, calls=%fused_computation.18 | convolution fusion | flops 2147483648 | bytes 11534336 | tf_op jit(solution)/shard_map/dot_general | solution.py:46
  39.1 0.0 all-gather.2.cloned.1.call-done
  39.1 0.0 copy-start
  39.1 7.4 %fusion.5 = f32[256,2048]{1,0:T(8,128)} fusion(bf16[256,2048]{1,0:T(8,128)(2,1)} %all-gather.2.cloned.1.call-done, bf16[2048,2048]{1,0:T(8,128)(2,1)} %param.7), kind=kOutput, calls=%fused_computation.20 | convolution fusion | flops 2147483648 | bytes 11534336 | tf_op jit(solution)/shard_map/dot_general | solution.py:67
  46.5 0.0 copy-done
  46.5 7.0 %fusion.4 = f32[256,2048]{1,0:T(8,128)} fusion(bf16[256,2048]{1,0:T(8,128)(2,1)S(1)} %copy-done, bf16[2048,2048]{1,0:T(8,128)(2,1)} %param.8), kind=kOutput, calls=%fused_computation.19 | convolution fusion | flops 2147483648 | bytes 11534336 | tf_op jit(solution)/shard_map/dot_general | solution.py:68
  53.6 0.0 all-reduce.3.cloned.1.call-update
  53.6 0.2 reduce-scatter.2.cloned.1.call-start
  53.8 225.3 %all-reduce.3.cloned.1.call-done = (f32[256,2048]{1,0:T(8,128)}, f32[256,2048]{1,0:T(8,128)}, f32[256,2048]{1,0:T(8,128)}) async-done(((f32[256,2048]{1,0:T(8,128)}, f32[256,2048]{1,0:T(8,128)}, f32[256,2048]{1,0:T(8,128)}), (f32[256,2048]{1,0:T(8,128)}, f32[256,2048]{1,0:T(8,128)}, f32[256,2048]{1,0:T(8,128)})) %all-reduce.3.cloned.1.call-update) | async-done | bytes 6291472 | tf_op jit(solution)/shard_map/psum | solution.py:70
  279.1 0.0 slice-start
  279.1 4.3 %multiply_convert_fusion.1 = (bf16[256,2048]{1,0:T(8,128)(2,1)S(1)}, bf16[256,2048]{1,0:T(8,128)(2,1)S(1)}) fusion(f32[256,2048]{1,0:T(8,128)} %get-tuple-element.9, f32[256,2048]{1,0:T(8,128)} %get-tuple-element.8, f32[256,2048]{1,0:T(8,128)} %get-tuple-element.10), kind=kLoop, calls=%fused_computation.5 | loop fusion | flops 6815744 | bytes 8388608 | tf_op jit(solution)/shard_map/convert_element_type | solution.py:58
  283.5 0.0 slice-start.1
  283.5 5.9 %fusion.6 = f32[256,2048]{1,0:T(8,128)S(1)} fusion(bf16[256,2048]{1,0:T(8,128)(2,1)S(1)} %get-tuple-element.12, bf16[2048,2048]{1,0:T(8,128)(2,1)} %param.7), kind=kOutput, calls=%fused_computation.21 | convolution fusion | flops 2147483648 | bytes 11534336 | tf_op jit(solution)/shard_map/dot_general | solution.py:46
  289.4 0.0 slice-done
  289.4 0.0 slice-done.1
  289.4 3.7 %convolution_add_fusion = f32[256,2048]{1,0:T(8,128)} fusion(f32[256,2048]{1,0:T(8,128)S(1)} %fusion.6, bf16[256,2048]{1,0:T(8,128)(2,1)S(1)} %get-tuple-element.11, bf16[2048,2048]{1,0:T(8,128)(2,1)S(1)} %bitcast.20), kind=kOutput, calls=%fused_computation.3 | convolution fusion | flops 2148007936 | bytes 13631488 | tf_op jit(solution)/shard_map/dot_general | solution.py:46
  293.1 0.0 reduce-scatter.2.cloned.1.call-update
  293.1 5.8 %convert_bitcast_fusion.1 = bf16[2048,2048]{0,1:T(8,128)(2,1)} fusion(bf16[256,2048]{1,0:T(8,128)(2,1)S(1)} %get-tuple-element.12, bf16[256,2048]{1,0:T(8,128)(2,1)S(1)} %copy-done), kind=kOutput, calls=%fused_computation.1 | convolution fusion | flops 2151677952 | bytes 10485760 | tf_op jit(solution)/shard_map/dot_general | solution.py:46
  298.9 12.4 %copy.9 = bf16[2048,2048]{1,0:T(8,128)(2,1)} copy(bf16[2048,2048]{0,1:T(8,128)(2,1)} %convert_bitcast_fusion.1) | data formatting | bytes 16777216
  311.3 5.8 %convert_bitcast_fusion = bf16[2048,2048]{0,1:T(8,128)(2,1)} fusion(bf16[256,2048]{1,0:T(8,128)(2,1)S(1)} %get-tuple-element.11, bf16[256,2048]{1,0:T(8,128)(2,1)S(1)} %copy-done), kind=kOutput, calls=%fused_computation | convolution fusion | flops 2151677952 | bytes 10485760 | tf_op jit(solution)/shard_map/dot_general | solution.py:46
  317.1 0.0 copy-start.1
  317.1 0.0 copy-start.3
  317.1 12.4 %copy.10 = bf16[2048,2048]{1,0:T(8,128)(2,1)} copy(bf16[2048,2048]{0,1:T(8,128)(2,1)} %convert_bitcast_fusion) | data formatting | bytes 16777216
  329.5 0.0 copy-done.1
  329.5 0.0 copy-done.3
  329.5 7.5 %convolution_convert_fusion = bf16[2048,2048]{1,0:T(8,128)(2,1)} fusion(bf16[256,2048]{1,0:T(8,128)(2,1)S(1)} %copy-done.3, f32[256,2048]{1,0:T(8,128)} %get-tuple-element.10, f32[256,2048]{1,0:T(8,128)S(1)} %copy-done.1), kind=kOutput, calls=%fused_computation.2 | convolution fusion | flops 2154823680 | bytes 13631488 | tf_op jit(solution)/shard_map/dot_general | solution.py:46
  337.0 0.0 reduce-scatter.2.cloned.1.call-done
  337.0 1.6 convert_element_type.29
  (8 shorter events, 0.1 us)
Async XLA Ops:
  7.2 31.9 %all-gather.2.cloned.1.call-start = ((), (), s32[]{:S(2)}) async-start(), calls=%async_computation.1 | async-start | bytes 1179648 | tf_op jit(solution)/shard_map/all_gather | solution.py:66
  7.2 6.3 %collective-permute-start = (bf16[32,2048]{1,0:T(8,128)(2,1)}, bf16[32,2048]{1,0:T(8,128)(2,1)S(1)}, u32[]{:S(2)}, u32[]{:S(2)}) collective-permute-start(bf16[32,2048]{1,0:T(8,128)(2,1)} %param.6), channel_id=1, source_target_pairs={{0,1},{1,2},{2,3},{3,4},{4,5},{5,6},{6,7},{7,0},{8,9},{9,10},{10,1... | collective-permute-start | bytes 393224 | tf_op jit(solution)/shard_map/ppermute | solution.py:29
  7.7 6.1 %collective-permute-start.1 = (bf16[32,2048]{1,0:T(8,128)(2,1)}, bf16[32,2048]{1,0:T(8,128)(2,1)S(1)}, u32[]{:S(2)}, u32[]{:S(2)}) collective-permute-start(bf16[32,2048]{1,0:T(8,128)(2,1)} %param.6), channel_id=1, source_target_pairs={{0,7},{1,0},{2,1},{3,2},{4,3},{5,4},{6,5},{7,6},{8,15},{9,8},{10,9... | collective-permute-start | bytes 393224 | tf_op jit(solution)/shard_map/ppermute | solution.py:34
  10.7 268.4 %all-reduce.3.cloned.1.call-start = ((), (), s32[]{:S(2)}) async-start(), calls=%async_computation.3 | async-start | bytes 12582912 | tf_op jit(solution)/shard_map/psum | solution.py:70
  13.5 5.3 %collective-permute-start.2 = (bf16[32,2048]{1,0:T(8,128)(2,1)S(1)}, bf16[32,2048]{1,0:T(8,128)(2,1)S(1)}, u32[]{:S(2)}, u32[]{:S(2)}) collective-permute-start(bf16[32,2048]{1,0:T(8,128)(2,1)S(1)} %collective-permute-done), channel_id=1, source_target_pairs={{0,1},{1,2},{2,3},{3,4},{4,5},{5,6},{6,7},{7,0},{8,9},{9,10},{10,1... | collective-permute-start | bytes 393224 | tf_op jit(solution)/shard_map/ppermute | solution.py:29
  13.8 5.2 %collective-permute-start.3 = (bf16[32,2048]{1,0:T(8,128)(2,1)S(1)}, bf16[32,2048]{1,0:T(8,128)(2,1)S(1)}, u32[]{:S(2)}, u32[]{:S(2)}) collective-permute-start(bf16[32,2048]{1,0:T(8,128)(2,1)S(1)} %collective-permute-done.1), channel_id=1, source_target_pairs={{0,7},{1,0},{2,1},{3,2},{4,3},{5,4},{6,5},{7,6},{8,15},{9,8},{10,9... | collective-permute-start | bytes 393224 | tf_op jit(solution)/shard_map/ppermute | solution.py:34
  18.8 7.0 %collective-permute-start.4 = (bf16[32,2048]{1,0:T(8,128)(2,1)S(1)}, bf16[32,2048]{1,0:T(8,128)(2,1)S(1)}, u32[]{:S(2)}, u32[]{:S(2)}) collective-permute-start(bf16[32,2048]{1,0:T(8,128)(2,1)S(1)} %collective-permute-done.2), channel_id=1, source_target_pairs={{0,1},{1,2},{2,3},{3,4},{4,5},{5,6},{6,7},{7,0},{8,9},{9,10},{10,1... | collective-permute-start | bytes 393224 | tf_op jit(solution)/shard_map/ppermute | solution.py:29
  19.1 6.7 %collective-permute-start.5 = (bf16[32,2048]{1,0:T(8,128)(2,1)S(1)}, bf16[32,2048]{1,0:T(8,128)(2,1)S(1)}, u32[]{:S(2)}, u32[]{:S(2)}) collective-permute-start(bf16[32,2048]{1,0:T(8,128)(2,1)S(1)} %collective-permute-done.3), channel_id=1, source_target_pairs={{0,7},{1,0},{2,1},{3,2},{4,3},{5,4},{6,5},{7,6},{8,15},{9,8},{10,9... | collective-permute-start | bytes 393224 | tf_op jit(solution)/shard_map/ppermute | solution.py:34
  25.7 5.3 %collective-permute-start.6 = (bf16[32,2048]{1,0:T(8,128)(2,1)S(1)}, bf16[32,2048]{1,0:T(8,128)(2,1)S(1)}, u32[]{:S(2)}, u32[]{:S(2)}) collective-permute-start(bf16[32,2048]{1,0:T(8,128)(2,1)S(1)} %collective-permute-done.4), channel_id=1, source_target_pairs={{0,1},{1,2},{2,3},{3,4},{4,5},{5,6},{6,7},{7,0},{8,9},{9,10},{10,1... | collective-permute-start | bytes 393224 | tf_op jit(solution)/shard_map/ppermute | solution.py:29
  31.0 1.0 copy-start.2
  39.1 7.4 %copy-start = (bf16[256,2048]{1,0:T(8,128)(2,1)S(1)}, bf16[256,2048]{1,0:T(8,128)(2,1)}, u32[]{:S(2)}) copy-start(bf16[256,2048]{1,0:T(8,128)(2,1)} %all-gather.2.cloned.1.call-done) | copy-start | bytes 3145732
  53.6 283.4 %reduce-scatter.2.cloned.1.call-start = ((), (), s32[]{:S(2)}) async-start(), calls=%async_computation.2 | async-start | bytes 2359296 | tf_op jit(solution)/shard_map/reduce_scatter | solution.py:75
  279.1 10.2 %slice-start = ((s8[8388608]{0:T(1024)(128)(4,1)}), s8[4194304]{0:T(1024)(128)(4,1)S(1)}, s32[]{:S(2)}) async-start(s8[8388608]{0:T(1024)(128)(4,1)} %bitcast.19), calls=%async_computation.4 | async-start | bytes 8388608
  283.5 5.9 %slice-start.1 = ((s8[8388608]{0:T(1024)(128)(4,1)}), s8[4194304]{0:T(1024)(128)(4,1)S(1)}, s32[]{:S(2)}) async-start(s8[8388608]{0:T(1024)(128)(4,1)} %bitcast.19), calls=%async_computation.5 | async-start | bytes 8388608
  317.1 12.4 %copy-start.1 = (f32[256,2048]{1,0:T(8,128)S(1)}, f32[256,2048]{1,0:T(8,128)}, u32[]{:S(2)}) copy-start(f32[256,2048]{1,0:T(8,128)} %get-tuple-element.8) | copy-start | bytes 6291460
  317.1 12.4 %copy-start.3 = (bf16[256,2048]{1,0:T(8,128)(2,1)S(1)}, bf16[256,2048]{1,0:T(8,128)(2,1)}, u32[]{:S(2)}) copy-start(bf16[256,2048]{1,0:T(8,128)(2,1)} %copy-done.2) | copy-start | bytes 3145732
Sparse Core Ops, SparseCore 0:
  10.8 26.4 all-gather.1
  53.7 225.3 all-reduce.2
  293.3 40.1 reduce-scatter.1
